TPU v7x, 512 devices: a whole 4x8x8 slice. The times are simulated.
512 devices in a mesh: ctx: 64 (over y, z_lo, x), mp: 8 (over z_hi, core).
Axes of the slice: x: 4, y: 8, z: 8 (z_hi: 4, z_lo: 2; z = z_hi * 2 + z_lo), core: 2. Of those that a mesh axis runs over, the one named last changes fastest.
Arguments:
- queries: bfloat16 [16384, 8192], P('ctx', 'mp'), may hold values from -6 to 6
- key_feats: bfloat16 [16384, 8192], P('ctx', 'mp'), may hold values from -6 to 6
- value_feats: bfloat16 [16384, 8192], P('ctx', 'mp'), may hold values from -6 to 6
- filters: bfloat16 [512, 128], P('mp'), may hold values from -0.5 to 0.5
- grad_out: bfloat16 [16384, 8192], P('ctx', 'mp'), may hold values from -40 to 40
Outputs:
- mixer_out: bfloat16 [16384, 8192], P('ctx', 'mp')
- grad_queries: bfloat16 [16384, 8192], P('ctx', 'mp')
- grad_keys: bfloat16 [16384, 8192], P('ctx', 'mp')
- grad_values: bfloat16 [16384, 8192], P('ctx', 'mp')
- grad_filters: float32 [512, 128], P('mp')
All inputs are finite; a program needn't handle non-finite values.
Results may differ from a plain program's by a relative error of at most 0.0058.
Values may be sent and summed in bfloat16 or wider, within the bound.
No kernel may reach another device: no remote copies, remote signals or barrier semaphores. Data moves between devices by JAX's collectives and lax.ppermute only.
A program may use at most 64 MiB of HBM per device.

v0:
```python
import jax
import jax.numpy as jnp
from jax import lax
from jax.sharding import PartitionSpec as P

D = 8192
G = 16


def contract(formula, first_op, second_op):
    return jnp.einsum(formula, first_op, second_op, preferred_element_type=jnp.float32)


def toeplitz(filt):
    count, filter_len = filt.shape
    flipped = filt[:, ::-1]
    lead_zero = jnp.zeros((count, 1), filt.dtype)
    trailing = jnp.zeros((count, filter_len), filt.dtype)
    pattern = jnp.concatenate([lead_zero, flipped, trailing], axis=1)
    repeated = jnp.tile(pattern, (1, filter_len))
    return repeated[:, : filter_len * 2 * filter_len].reshape(count, filter_len, 2 * filter_len)


def make_windows(blocks, before):
    earlier = jnp.concatenate([before[:, :, None, :], blocks[:, :, :-1, :]], axis=2)
    return jnp.concatenate([earlier, blocks], axis=3)


def forward_conv(signal, before, toeplitz_mat):
    groups_here, group_size, seq_len = signal.shape
    filter_len = toeplitz_mat.shape[1]
    blocks = signal.reshape(groups_here, group_size, seq_len // filter_len, filter_len)
    window_rows = make_windows(blocks, before)
    result = contract("gam,gsnm->gsna", toeplitz_mat, window_rows)
    return (result.reshape(groups_here, group_size, seq_len), window_rows)


def backward_conv(grad_rows, after, toeplitz_mat):
    groups_here, group_size, seq_len = grad_rows.shape
    filter_len = toeplitz_mat.shape[1]
    blocks = grad_rows.reshape(groups_here, group_size, seq_len // filter_len, filter_len)
    spread = contract("gam,gsna->gsnm", toeplitz_mat, blocks)
    tail_part = contract("gam,gsa->gsm", toeplitz_mat, after)
    next_part = jnp.concatenate(
        [spread[:, :, 1:, :filter_len], tail_part[:, :, None, :filter_len]], axis=2
    )
    return (spread[:, :, :, filter_len:] + next_part).reshape(groups_here, group_size, seq_len)


def filter_grad(grad_rows, window_rows, filter_len):
    groups_here, group_size, seq_len = grad_rows.shape
    blocks = grad_rows.reshape(groups_here, group_size, seq_len // filter_len, filter_len)
    correlate = contract("gsna,gsnm->gam", blocks, window_rows)
    flattened = correlate.reshape(groups_here, filter_len * 2 * filter_len)
    flattened = jnp.concatenate(
        [flattened, jnp.zeros((groups_here, filter_len), jnp.float32)], axis=1
    )
    flattened = flattened.reshape(groups_here, filter_len, 2 * filter_len + 1)
    diagonals = jnp.sum(flattened, axis=1)
    return diagonals[:, 1 : filter_len + 1][:, ::-1]


def shards(queries, key_feats, value_feats, filters, grad_out):
    tokens, channels = queries.shape
    slab_groups, filter_len = filters.shape
    product = (
        (key_feats.astype(jnp.float32) * value_feats.astype(jnp.float32)).astype(jnp.bfloat16).T
    )
    grad_mix = (grad_out.astype(jnp.float32) * queries.astype(jnp.float32)).astype(jnp.bfloat16).T
    owners = lax.axis_size("ctx")
    own_width = channels // owners
    own_groups = own_width // G
    signal = lax.all_to_all(product, "ctx", split_axis=0, concat_axis=1, tiled=True)
    grad_rows = lax.all_to_all(grad_mix, "ctx", split_axis=0, concat_axis=1, tiled=True)
    seq_len = signal.shape[1]
    signal = signal.reshape(own_groups, G, seq_len)
    grad_rows = grad_rows.reshape(own_groups, G, seq_len)
    first_group = lax.axis_index("ctx") * own_groups
    own_filters = lax.dynamic_slice_in_dim(filters, first_group, own_groups, 0)
    toeplitz_mat = toeplitz(own_filters)
    zero_rim = jnp.zeros((own_groups, G, filter_len), jnp.bfloat16)
    conv_out, window_rows = forward_conv(signal, zero_rim, toeplitz_mat)
    conv_out = conv_out.astype(jnp.bfloat16).reshape(own_width, seq_len)
    conv_grad = (
        backward_conv(grad_rows, zero_rim, toeplitz_mat)
        .astype(jnp.bfloat16)
        .reshape(own_width, seq_len)
    )
    partial_grad = filter_grad(grad_rows, window_rows, filter_len)
    conv_rows = lax.all_to_all(conv_out, "ctx", split_axis=1, concat_axis=0, tiled=True)
    grad_back = lax.all_to_all(conv_grad, "ctx", split_axis=1, concat_axis=0, tiled=True)
    raw_filters = lax.all_gather(partial_grad, "ctx", axis=0, tiled=True)
    conv_f = conv_rows.T.astype(jnp.float32)
    back_f = grad_back.T.astype(jnp.float32)
    mixer_out = (queries.astype(jnp.float32) * conv_f).astype(jnp.bfloat16)
    grad_queries = (grad_out.astype(jnp.float32) * conv_f).astype(jnp.bfloat16)
    grad_keys = (back_f * value_feats.astype(jnp.float32)).astype(jnp.bfloat16)
    grad_values = (back_f * key_feats.astype(jnp.float32)).astype(jnp.bfloat16)
    square_sum = lax.psum(jnp.sum(raw_filters * raw_filters), "mp")
    grad_rms = jnp.sqrt(square_sum / (D // G * filter_len) + 1e-06)
    grad_filters = raw_filters * jnp.minimum(1.0, 1.0 / grad_rms)
    return (mixer_out, grad_queries, grad_keys, grad_values, grad_filters)


def solution(mesh):
    placed = (P("ctx", "mp"), P("ctx", "mp"), P("ctx", "mp"), P("mp", None), P("ctx", "mp"))
    return jax.shard_map(
        shards,
        mesh=mesh,
        in_specs=placed,
        out_specs=(P("ctx", "mp"), P("ctx", "mp"), P("ctx", "mp"), P("ctx", "mp"), P("mp", None)),
        check_vma=False,
    )
```

profile of v0, /device:TPU:1, one launch (start us, length us, event | category | flops | bytes accessed | tf_op | source)
XLA Modules:
  0.0 278.9 jit_solution(11719873778474944530)
XLA Ops:
  0.6 0.0 copy-start
  0.6 1.2 copy.28
  1.9 1.2 copy.33
  3.1 0.9 fusion.6
  4.1 12.9 %all-to-all-start.2 = ((bf16[64,16,256]{2,1,0:T(8,128)(2,1)}), bf16[64,16,256]{2,1,0:T(8,128)(2,1)S(1)}, u32[]{:S(2)}, u32[]{:S(2)}) async-start(bf16[64,16,256]{2,1,0:T(8,128)(2,1)} %bitcast.10), calls=%async_computation.2 | async-start | bytes 1048576 | tf_op jit(solution)/shard_map/all_to_all | solution.py:74
  17.0 0.0 copy-done
  17.0 0.1 rev.6
  17.1 0.1 pad.6.clone
  17.2 0.1 fusion.13
  17.3 0.4 tile.13
  17.7 0.4 slice_reduce_fusion
  18.2 0.1 convolution_bitcast_fusion.2
  18.3 14.5 %all-to-all-done.2 = bf16[64,16,256]{2,1,0:T(8,128)(2,1)S(1)} async-done(((bf16[64,16,256]{2,1,0:T(8,128)(2,1)}), bf16[64,16,256]{2,1,0:T(8,128)(2,1)S(1)}, u32[]{:S(2)}, u32[]{:S(2)}) %all-to-all-start.2) | async-done | bytes 524320 | tf_op jit(solution)/shard_map/all_to_all | solution.py:74
  32.8 0.2 copy.34
  32.9 0.2 reshape.85
  33.1 0.4 convolution_bitcast_fusion
  33.5 0.1 slice.27
  33.6 0.1 fusion.9
  33.8 0.0 copy-start.1
  33.8 0.2 convert_element_type.93
  34.0 1.1 copy.35
  35.0 0.0 copy-start.2
  35.0 7.2 %all-to-all-start.3 = ((bf16[16,64,256]{2,0,1:T(8,128)(2,1)}), bf16[16,64,256]{2,0,1:T(8,128)(2,1)S(1)}, u32[]{:S(2)}, u32[]{:S(2)}) async-start(bf16[16,64,256]{2,0,1:T(8,128)(2,1)} %copy.35), calls=%async_computation.3 | async-start | bytes 1048576 | tf_op jit(solution)/shard_map/all_to_all | solution.py:91
  42.2 0.0 copy-done.1
  42.2 1.0 copy.29
  43.2 0.0 copy-done.2
  43.2 1.0 copy.30
  44.2 12.8 %all-to-all-done.3 = bf16[16,64,256]{2,0,1:T(8,128)(2,1)S(1)} async-done(((bf16[16,64,256]{2,0,1:T(8,128)(2,1)}), bf16[16,64,256]{2,0,1:T(8,128)(2,1)S(1)}, u32[]{:S(2)}, u32[]{:S(2)}) %all-to-all-start.3) | async-done | bytes 524320 | tf_op jit(solution)/shard_map/all_to_all | solution.py:91
  57.0 1.5 fusion.2
  58.5 21.8 %all_to_all.52 = bf16[64,16,256]{2,1,0:T(8,128)(2,1)S(1)} all-to-all(bf16[64,16,256]{2,1,0:T(8,128)(2,1)S(1)} %bitcast.50), channel_id=1, replica_groups=mesh['ctx'=64,'mp'=8] {'ctx'}, dimensions={0} | all-to-all | bytes 1048576 | tf_op jit(solution)/shard_map/all_to_all | solution.py:73
  80.4 0.2 copy.31
  80.5 1.0 reshape_reshape.2
  81.5 2.4 convolution_convert_fusion
  83.9 1.2 convert_element_type.83
  85.1 1.1 copy.32
  86.2 8.1 %all-to-all-start.1 = ((bf16[16,64,256]{2,0,1:T(8,128)(2,1)}), bf16[16,64,256]{2,0,1:T(8,128)(2,1)S(1)}, u32[]{:S(2)}, u32[]{:S(2)}) async-start(bf16[16,64,256]{2,0,1:T(8,128)(2,1)} %copy.32), calls=%async_computation.1 | async-start | bytes 1048576 | tf_op jit(solution)/shard_map/all_to_all | solution.py:90
  94.4 1.0 copy.39
  95.4 1.5 convolution_bitcast_fusion.1
  96.9 0.1 copy.42
  97.1 0.3 pad_reduce_fusion
  97.4 0.3 reshape.87
  97.8 0.1 slice.29
  97.8 0.1 rev.7
  97.9 127.5 %all-gather = f32[64,1,128]{2,1,0:T(1,128)S(1)} all-gather(f32[1,1,128]{2,1,0:T(1,128)S(1)} %bitcast.57), channel_id=1, replica_groups=mesh['ctx'=64,'mp'=8] {'ctx'}, dimensions={0}, use_global_device_ids=true | all-gather | bytes 33280 | tf_op jit(solution)/shard_map/all_gather | solution.py:92
  225.5 0.7 multiply_reduce_fusion
  226.1 1.0 copy.40
  227.1 48.2 %psum.7 = f32[]{:T(128)} all-reduce(f32[]{:T(128)} %multiply_reduce_fusion), channel_id=1, replica_groups=mesh['ctx'=64,'mp'=8] {'mp'}, use_global_device_ids=true, to_apply=%region_2.0 | all-reduce | flops 1 | bytes 8 | tf_op jit(solution)/shard_map/psum | solution.py:99
  276.0 0.6 broadcast_multiply_fusion
  276.6 0.0 all-to-all-done.1
  276.6 0.2 fusion.5
  276.9 1.0 copy.37
  277.9 1.0 copy.38
  (8 shorter events, 0.1 us)
Async XLA Ops:
  0.6 16.4 %copy-start = (bf16[64,128]{1,0:T(8,128)(2,1)S(1)}, bf16[64,128]{1,0:T(8,128)(2,1)}, u32[]{:S(2)}) copy-start(bf16[64,128]{1,0:T(8,128)(2,1)} %param.8) | copy-start | bytes 49156
  4.1 28.7 %all-to-all-start.2 = ((bf16[64,16,256]{2,1,0:T(8,128)(2,1)}), bf16[64,16,256]{2,1,0:T(8,128)(2,1)S(1)}, u32[]{:S(2)}, u32[]{:S(2)}) async-start(bf16[64,16,256]{2,1,0:T(8,128)(2,1)} %bitcast.10), calls=%async_computation.2 | async-start | bytes 1048576 | tf_op jit(solution)/shard_map/all_to_all | solution.py:74
  33.8 8.5 %copy-start.1 = (bf16[256,1024]{1,0:T(8,128)(2,1)S(1)}, bf16[256,1024]{1,0:T(8,128)(2,1)}, u32[]{:S(2)}) copy-start(bf16[256,1024]{1,0:T(8,128)(2,1)} %param.6) | copy-start | bytes 1572868
  35.0 8.2 %copy-start.2 = (bf16[256,1024]{1,0:T(8,128)(2,1)S(1)}, bf16[256,1024]{1,0:T(8,128)(2,1)}, u32[]{:S(2)}) copy-start(bf16[256,1024]{1,0:T(8,128)(2,1)} %param.7) | copy-start | bytes 1572868
  35.0 22.0 %all-to-all-start.3 = ((bf16[16,64,256]{2,0,1:T(8,128)(2,1)}), bf16[16,64,256]{2,0,1:T(8,128)(2,1)S(1)}, u32[]{:S(2)}, u32[]{:S(2)}) async-start(bf16[16,64,256]{2,0,1:T(8,128)(2,1)} %copy.35), calls=%async_computation.3 | async-start | bytes 1048576 | tf_op jit(solution)/shard_map/all_to_all | solution.py:91
  86.2 190.4 %all-to-all-start.1 = ((bf16[16,64,256]{2,0,1:T(8,128)(2,1)}), bf16[16,64,256]{2,0,1:T(8,128)(2,1)S(1)}, u32[]{:S(2)}, u32[]{:S(2)}) async-start(bf16[16,64,256]{2,0,1:T(8,128)(2,1)} %copy.32), calls=%async_computation.1 | async-start | bytes 1048576 | tf_op jit(solution)/shard_map/all_to_all | solution.py:90
where the time goes:
time: 279 us
  blocking collectives  198 us (71%)
  starting transfers between devices  28.2 us (10%)
  waiting for transfers between devices  27.3 us (10%)
  local copies, waits for them, and re-layouts  15.6 us (6%)
  matrix products  4.52 us (2%)
  other arithmetic  4.21 us (2%)
    all_gather x1, blocking collectives, shards(): raw_filters = lax.all_gather(partial_grad, 'ctx', axis=0, tiled=True)  128 us
    psum x1, blocking collectives, shards(): square_sum = lax.psum(jnp.sum(raw_filters * raw_filters), 'mp')  48.2 us
    all_to_all x1, blocking collectives, shards(): lax.all_to_all(product, 'ctx', split_axis=0, concat_axis=1, tiled=True)  21.8 us
    all_to_all x1, waiting for transfers between devices, shards(): lax.all_to_all(grad_mix, 'ctx', split_axis=0, concat_axis=1, tiled=True)  14.5 us
    all_to_all x1, starting transfers between devices, shards(): lax.all_to_all(grad_mix, 'ctx', split_axis=0, concat_axis=1, tiled=True)  12.9 us
    all_to_all x1, waiting for transfers between devices, shards(): lax.all_to_all(conv_grad, 'ctx', split_axis=1, concat_axis=0, tiled=True)  12.8 us
    unnamed x15, local copies, waits for them, and re-layouts  8.66 us
    all_to_all x1, starting transfers between devices, shards(): lax.all_to_all(conv_out, 'ctx', split_axis=1, concat_axis=0, tiled=True)  8.11 us
  transfers between devices with their start and end apart: 3, of which 2 were waited for; matrix products, arithmetic and copies ran while one was open for 3% of the time, Pallas kernels for 0%

commit v1 on v0

--- a/solution.py
+++ b/solution.py
@@ -87,7 +87,10 @@
         .reshape(own_width, seq_len)
     )
     partial_grad = filter_grad(grad_rows, window_rows, filter_len)
-    conv_rows = lax.all_to_all(conv_out, "ctx", split_axis=1, concat_axis=0, tiled=True)
+    conv_rows = jnp.concatenate(
+        lax.all_to_all(jnp.stack(jnp.split(conv_out, lax.axis_size("ctx"), axis=1)), "ctx", 0, 0),
+        axis=0,
+    )
     grad_back = lax.all_to_all(conv_grad, "ctx", split_axis=1, concat_axis=0, tiled=True)
     raw_filters = lax.all_gather(partial_grad, "ctx", axis=0, tiled=True)
     conv_f = conv_rows.T.astype(jnp.float32)

time: 279 us -> 315 us (1.13)
  local copies, waits for them, and re-layouts: 15.6 us -> 53.1 us
    unnamed x15 -> x77, local copies, waits for them, and re-layouts: 8.66 us -> 47.8 us
where the time goes in v1:
time: 315 us; the launch traced here: 314 us
  blocking collectives  198 us (63%)
  local copies, waits for them, and re-layouts  53.1 us (17%)
  starting transfers between devices  28.1 us (9%)
  waiting for transfers between devices  26.2 us (8%)
  other arithmetic  4.25 us (1%)
  matrix products  3.72 us (1%)
    all_gather x1, blocking collectives, shards(): raw_filters = lax.all_gather(partial_grad, 'ctx', axis=0, tiled=True)  128 us
    psum x1, blocking collectives, shards(): square_sum = lax.psum(jnp.sum(raw_filters * raw_filters), 'mp')  48.2 us
    unnamed x77, local copies, waits for them, and re-layouts  47.8 us
    all_to_all x1, blocking collectives, shards(): lax.all_to_all(product, 'ctx', split_axis=0, concat_axis=1, tiled=True)  21.8 us
    all_to_all x1, waiting for transfers between devices, shards(): lax.all_to_all(grad_mix, 'ctx', split_axis=0, concat_axis=1, tiled=True)  14.5 us
    all_to_all x1, starting transfers between devices, shards(): lax.all_to_all(grad_mix, 'ctx', split_axis=0, concat_axis=1, tiled=True)  12.9 us
    all_to_all x1, waiting for transfers between devices, shards(): lax.all_to_all(conv_grad, 'ctx', split_axis=1, concat_axis=0, tiled=True)  11.8 us
    all_to_all x1, starting transfers between devices, shards(): lax.all_to_all(jnp.stack(jnp.split(conv_out, lax.axis_size('ctx'), axis=1...  8.1 us
  transfers between devices with their start and end apart: 3, of which 2 were waited for; matrix products, arithmetic and copies ran while one was open for 3% of the time, Pallas kernels for 0%

profile of v1, /device:TPU:1, one launch (start us, length us, event | category | flops | bytes accessed | tf_op | source)
XLA Modules:
  0.0 314.4 jit_solution(3341216561655405164)
XLA Ops:
  0.6 1.2 copy.27
  1.9 1.2 copy.31
  3.1 0.9 fusion.6
  4.1 12.9 %all-to-all-start.2 = ((bf16[64,16,256]{2,1,0:T(8,128)(2,1)}), bf16[64,16,256]{2,1,0:T(8,128)(2,1)S(1)}, u32[]{:S(2)}, u32[]{:S(2)}) async-start(bf16[64,16,256]{2,1,0:T(8,128)(2,1)} %bitcast.72), calls=%async_computation.2 | async-start | bytes 1048576 | tf_op jit(solution)/shard_map/all_to_all | solution.py:74
  18.3 14.5 %all-to-all-done.2 = bf16[64,16,256]{2,1,0:T(8,128)(2,1)S(1)} async-done(((bf16[64,16,256]{2,1,0:T(8,128)(2,1)}), bf16[64,16,256]{2,1,0:T(8,128)(2,1)S(1)}, u32[]{:S(2)}, u32[]{:S(2)}) %all-to-all-start.2) | async-done | bytes 524320 | tf_op jit(solution)/shard_map/all_to_all | solution.py:74
  34.0 1.1 copy.33
  35.0 7.0 %all-to-all-start.3 = ((bf16[16,64,256]{2,0,1:T(8,128)(2,1)}), bf16[16,64,256]{2,0,1:T(8,128)(2,1)S(1)}, u32[]{:S(2)}, u32[]{:S(2)}) async-start(bf16[16,64,256]{2,0,1:T(8,128)(2,1)} %copy.33), calls=%async_computation.3 | async-start | bytes 1048576 | tf_op jit(solution)/shard_map/all_to_all | solution.py:94
  42.1 1.0 copy.28
  43.1 2.0 copy.29
  45.1 11.8 %all-to-all-done.3 = bf16[16,64,256]{2,0,1:T(8,128)(2,1)S(1)} async-done(((bf16[16,64,256]{2,0,1:T(8,128)(2,1)}), bf16[16,64,256]{2,0,1:T(8,128)(2,1)S(1)}, u32[]{:S(2)}, u32[]{:S(2)}) %all-to-all-start.3) | async-done | bytes 524320 | tf_op jit(solution)/shard_map/all_to_all | solution.py:94
  56.9 1.5 fusion.2
  58.4 21.8 %all_to_all.47 = bf16[64,16,256]{2,1,0:T(8,128)(2,1)S(1)} all-to-all(bf16[64,16,256]{2,1,0:T(8,128)(2,1)S(1)} %bitcast.313), channel_id=1, replica_groups=mesh['ctx'=64,'mp'=8] {'ctx'}, dimensions={0} | all-to-all | bytes 1048576 | tf_op jit(solution)/shard_map/all_to_all | solution.py:73
  80.4 1.0 reshape_reshape.2
  81.4 1.6 convolution_convert_fusion
  83.3 0.6 constant_dynamic-update-slice_fusion.63
  84.0 0.6 constant_dynamic-update-slice_fusion.62
  84.5 0.6 constant_dynamic-update-slice_fusion.61
  85.2 0.6 constant_dynamic-update-slice_fusion.60
  85.8 0.6 constant_dynamic-update-slice_fusion.59
  86.3 0.6 constant_dynamic-update-slice_fusion.58
  87.0 0.6 constant_dynamic-update-slice_fusion.57
  87.5 0.6 constant_dynamic-update-slice_fusion.56
  88.2 0.6 constant_dynamic-update-slice_fusion.55
  88.8 0.6 constant_dynamic-update-slice_fusion.54
  89.3 0.6 constant_dynamic-update-slice_fusion.53
  90.0 0.6 constant_dynamic-update-slice_fusion.52
  90.5 0.6 constant_dynamic-update-slice_fusion.51
  91.2 0.6 constant_dynamic-update-slice_fusion.50
  91.8 0.6 constant_dynamic-update-slice_fusion.49
  92.3 0.6 constant_dynamic-update-slice_fusion.48
  93.0 0.6 constant_dynamic-update-slice_fusion.47
  93.5 0.6 constant_dynamic-update-slice_fusion.46
  94.2 0.6 constant_dynamic-update-slice_fusion.45
  94.8 0.6 constant_dynamic-update-slice_fusion.44
  95.3 0.6 constant_dynamic-update-slice_fusion.43
  96.0 0.6 constant_dynamic-update-slice_fusion.42
  96.5 0.6 constant_dynamic-update-slice_fusion.41
  97.2 0.6 constant_dynamic-update-slice_fusion.40
  97.8 0.6 constant_dynamic-update-slice_fusion.39
  98.3 0.6 constant_dynamic-update-slice_fusion.38
  99.0 0.6 constant_dynamic-update-slice_fusion.37
  99.5 0.6 constant_dynamic-update-slice_fusion.36
  100.2 0.6 constant_dynamic-update-slice_fusion.35
  100.8 0.6 constant_dynamic-update-slice_fusion.34
  101.3 0.6 constant_dynamic-update-slice_fusion.33
  102.0 0.6 constant_dynamic-update-slice_fusion.32
  102.5 0.6 constant_dynamic-update-slice_fusion.31
  103.2 0.6 constant_dynamic-update-slice_fusion.30
  103.8 0.6 constant_dynamic-update-slice_fusion.29
  104.3 0.6 constant_dynamic-update-slice_fusion.28
  105.0 0.6 constant_dynamic-update-slice_fusion.27
  105.5 0.6 constant_dynamic-update-slice_fusion.26
  106.2 0.6 constant_dynamic-update-slice_fusion.25
  106.8 0.6 constant_dynamic-update-slice_fusion.24
  121.8 8.1 %all-to-all-start.1 = ((bf16[64,16,256]{2,1,0:T(8,128)(2,1)}), bf16[64,16,256]{2,1,0:T(8,128)(2,1)S(1)}, u32[]{:S(2)}, u32[]{:S(2)}) async-start(bf16[64,16,256]{2,1,0:T(8,128)(2,1)} %constant_dynamic-update-slice_fusion), calls=%async_computation.1 | async-start | bytes 1048576 | tf_op jit(solution)/shard_map/all_to_all | solution.py:91
  129.9 1.0 copy.37
  130.9 1.5 convolution_bitcast_fusion.1
  133.5 127.5 %all-gather = f32[64,1,128]{2,1,0:T(1,128)S(1)} all-gather(f32[1,1,128]{2,1,0:T(1,128)S(1)} %bitcast.385), channel_id=1, replica_groups=mesh['ctx'=64,'mp'=8] {'ctx'}, dimensions={0}, use_global_device_ids=true | all-gather | bytes 33280 | tf_op jit(solution)/shard_map/all_gather | solution.py:95
  261.0 0.7 multiply_reduce_fusion
  261.6 1.0 copy.38
  262.6 48.2 %psum.7 = f32[]{:T(128)} all-reduce(f32[]{:T(128)} %multiply_reduce_fusion), channel_id=1, replica_groups=mesh['ctx'=64,'mp'=8] {'mp'}, use_global_device_ids=true, to_apply=%region_2.0 | all-reduce | flops 1 | bytes 8 | tf_op jit(solution)/shard_map/psum | solution.py:102
  311.5 0.6 broadcast_multiply_fusion
  312.4 1.0 copy.35
  313.4 1.0 copy.36
  (57 shorter events, 18.6 us)
Async XLA Ops:
  0.6 16.4 %copy-start = (bf16[64,128]{1,0:T(8,128)(2,1)S(1)}, bf16[64,128]{1,0:T(8,128)(2,1)}, u32[]{:S(2)}) copy-start(bf16[64,128]{1,0:T(8,128)(2,1)} %param.8) | copy-start | bytes 49156
  4.1 28.7 %all-to-all-start.2 = ((bf16[64,16,256]{2,1,0:T(8,128)(2,1)}), bf16[64,16,256]{2,1,0:T(8,128)(2,1)S(1)}, u32[]{:S(2)}, u32[]{:S(2)}) async-start(bf16[64,16,256]{2,1,0:T(8,128)(2,1)} %bitcast.72), calls=%async_computation.2 | async-start | bytes 1048576 | tf_op jit(solution)/shard_map/all_to_all | solution.py:74
  33.9 8.1 %copy-start.1 = (bf16[256,1024]{1,0:T(8,128)(2,1)S(1)}, bf16[256,1024]{1,0:T(8,128)(2,1)}, u32[]{:S(2)}) copy-start(bf16[256,1024]{1,0:T(8,128)(2,1)} %param.6) | copy-start | bytes 1572868
  35.0 21.8 %all-to-all-start.3 = ((bf16[16,64,256]{2,0,1:T(8,128)(2,1)}), bf16[16,64,256]{2,0,1:T(8,128)(2,1)S(1)}, u32[]{:S(2)}, u32[]{:S(2)}) async-start(bf16[16,64,256]{2,0,1:T(8,128)(2,1)} %copy.33), calls=%async_computation.3 | async-start | bytes 1048576 | tf_op jit(solution)/shard_map/all_to_all | solution.py:94
  121.8 190.4 %all-to-all-start.1 = ((bf16[64,16,256]{2,1,0:T(8,128)(2,1)}), bf16[64,16,256]{2,1,0:T(8,128)(2,1)S(1)}, u32[]{:S(2)}, u32[]{:S(2)}) async-start(bf16[64,16,256]{2,1,0:T(8,128)(2,1)} %constant_dynamic-update-slice_fusion), calls=%async_computation.1 | async-start | bytes 1048576 | tf_op jit(solution)/shard_map/all_to_all | solution.py:91
